TPU v7x, 128 devices: a whole 4x4x4 slice. The times are simulated.
128 devices in a mesh: row: 8 (over y, core), col: 16 (over x, z).
Axes of the slice: x: 4, y: 4, z: 4, core: 2. Of those that a mesh axis runs over, the one named last changes fastest.
Arguments:
- descriptors: bfloat16 [16384, 1024], P(('row', 'col'))
- gradients: bfloat16 [3, 4, 16384, 1024], P(None, None, ('row', 'col'))
- sparse_panel: bfloat16 [512, 1024], P('col')
- sparse_trail: bfloat16 [2048, 1024], P('col')
- atom_counts: int32 [128, 8], P(('row', 'col')), may hold values from 1 to 16, 64 in all within a row
- owner_rows: int32 [128, 8], P(('row', 'col')), may hold values from 0 to 7, each once within a row
- neighbor_ids: int32 [1024, 16, 4], P(('row', 'col')), may hold values from 0 to 65519
Outputs:
- panel_factor: float32 [512, 512], replicated
- cross_factor: float32 [2048, 512], P('col')
- trail_residual: float32 [2048, 65536], P('col', 'row')
Inputs may be any that keep to these rules, and one draw needn't show every extreme that they name: `atom_counts`: the structures of one device's line hold 64 atoms together, and every line has a structure of 16 atoms. `owner_rows`: every device gives exactly one structure to each row group.
All inputs are finite; a program needn't handle non-finite values.
Results may differ from a plain program's by a relative error of at most 0.0043.
Values may be sent and summed in bfloat16 or wider, within the bound.
No kernel may reach another device: no remote copies, remote signals or barrier semaphores. Data moves between devices by JAX's collectives and lax.ppermute only.
A program may use at most 128 MiB of HBM per device.

v0:
```python
import jax
import jax.numpy as jnp
from jax import lax
from jax.sharding import PartitionSpec as P

ridge_value = 0.1


def slot_rows(environments, desc_here, slope_here, count_here, neighbor_here, owner_here):
    struct_count = count_here.shape[0]
    atom_slots = neighbor_here.shape[1]
    neighbor_count = neighbor_here.shape[2]
    env_count = environments.shape[0]
    correlation = lax.dot_general(
        environments, desc_here, (((1,), (1,)), ((), ())), preferred_element_type=jnp.float32
    )
    slope_dots = lax.dot_general(
        environments, slope_here, (((1,), (1,)), ((), ())), preferred_element_type=jnp.float32
    )
    slope_dots = slope_dots.reshape(env_count, 3, neighbor_count, struct_count, atom_slots)
    slot_index = jnp.arange(atom_slots, dtype=jnp.int32)
    live_mask = (slot_index[None, :] < count_here[:, None]).astype(jnp.float32)
    squares = (correlation * correlation).reshape(env_count, struct_count, atom_slots)
    energy = jnp.sum(squares * live_mask[None], axis=2) / count_here.astype(jnp.float32)[None, :]
    partner = neighbor_here % count_here[:, None, None]
    struct_index = jnp.arange(struct_count, dtype=jnp.int32)
    flat_index = (struct_index[:, None, None] * atom_slots + partner).reshape(-1)
    picked = jnp.take(correlation, flat_index, axis=1).reshape(
        env_count, struct_count, atom_slots, neighbor_count
    )
    picked = jnp.transpose(picked, (0, 3, 1, 2))
    forces = -2.0 * jnp.sum(picked[:, None] * slope_dots, axis=2) * live_mask[None, None]
    forces = jnp.transpose(forces, (0, 2, 3, 1)).reshape(env_count, struct_count, 3 * atom_slots)
    padding = jnp.zeros((env_count, struct_count, atom_slots - 1), jnp.float32)
    slot_values = jnp.concatenate([energy[:, :, None], forces, padding], axis=2).astype(
        jnp.bfloat16
    )
    chosen = (owner_here[None, :] == struct_index[:, None]).astype(jnp.int32)
    owner_order = jnp.sum(struct_index[None, :] * chosen, axis=1)
    return jnp.take(slot_values, owner_order, axis=1)


def factor_panel(gram_sum, cross_sum, total_rows):
    gram_matrix = gram_sum / total_rows + ridge_value * jnp.eye(
        gram_sum.shape[0], dtype=jnp.float32
    )
    lower_factor = jnp.linalg.cholesky(gram_matrix)
    coupling = lax.linalg.triangular_solve(
        lower_factor, cross_sum / total_rows, left_side=True, lower=True
    )
    weights = lax.linalg.triangular_solve(
        lower_factor, coupling, left_side=True, lower=True, transpose_a=True
    )
    return (lower_factor.T, coupling, weights)


def split_weights(weights):
    weight_high = weights.astype(jnp.bfloat16)
    held_high = lax.optimization_barrier(weight_high)
    weight_low = (weights - held_high.astype(jnp.float32)).astype(jnp.bfloat16)
    return (weight_high, weight_low)


def reduce_products(gram_part, cross_part):
    return lax.psum((gram_part, cross_part), ("row", "col"))


def contract_rows(left_side, right_side):
    return lax.dot_general(
        left_side, right_side, (((1,), (1,)), ((), ())), preferred_element_type=jnp.float32
    )


def contract_cols(left_side, right_side):
    return lax.dot_general(
        left_side, right_side, (((0,), (0,)), ((), ())), preferred_element_type=jnp.float32
    )


def arrange_direct(block_rows, row_count, col_count):
    env_width = block_rows.shape[0] // col_count
    slot_count = block_rows.shape[2]
    shaped = block_rows.reshape(col_count, env_width, row_count, slot_count)
    return jnp.transpose(shaped, (2, 0, 1, 3)).reshape(row_count * col_count, env_width, slot_count)


def restore_direct(block_rows, row_count, col_count):
    env_width = block_rows.shape[1]
    slot_count = block_rows.shape[2]
    shaped = block_rows.reshape(row_count, col_count, env_width, slot_count)
    return jnp.transpose(shaped, (2, 1, 0, 3)).reshape(
        env_width, row_count * col_count * slot_count
    )


def per_device(
    descriptors, gradients, sparse_panel, sparse_trail, atom_counts, owner_rows, neighbor_ids
):
    row_count = lax.axis_size("row")
    col_count = lax.axis_size("col")
    col_index = lax.axis_index("col")
    count_here = atom_counts[0]
    owner_here = owner_rows[0]
    slope_here = gradients.reshape(-1, gradients.shape[3])
    panel_width = sparse_panel.shape[0]
    trail_width = sparse_trail.shape[0]
    panel_total = panel_width * col_count
    trail_total = trail_width * col_count
    slot_count = 4 * neighbor_ids.shape[1]
    total_rows = row_count * row_count * col_count * slot_count
    own_envs = jnp.concatenate([sparse_panel, sparse_trail], axis=0)
    kernel_rows = slot_rows(
        lax.all_gather(own_envs, "col", axis=0, tiled=True),
        descriptors,
        slope_here,
        count_here,
        neighbor_ids,
        owner_here,
    )
    blocks = kernel_rows.reshape(col_count, panel_width + trail_width, row_count, slot_count)
    panel_rows = blocks[:, :panel_width].reshape(panel_total, row_count, slot_count)
    trail_rows = blocks[:, panel_width:].reshape(trail_total, row_count, slot_count)
    received = (
        lax.all_to_all(
            arrange_direct(panel_rows, row_count, col_count),
            ("row", "col"),
            split_axis=0,
            concat_axis=0,
            tiled=True,
        ),
        lax.all_to_all(
            arrange_direct(trail_rows, row_count, col_count),
            ("row", "col"),
            split_axis=0,
            concat_axis=0,
            tiled=True,
        ),
    )
    panel_own = restore_direct(received[0], row_count, col_count)
    trail_own = restore_direct(received[1], row_count, col_count)
    segment = lax.all_gather(panel_own, "col", axis=0, tiled=True)
    columns = jnp.concatenate(
        [contract_rows(segment, panel_own), contract_rows(segment, trail_own)], axis=1
    )
    gram_part = lax.dynamic_update_slice(
        jnp.zeros((panel_total, panel_total), jnp.float32),
        columns[:, :panel_width],
        (0, col_index * panel_width),
    )
    cross_part = lax.dynamic_update_slice(
        jnp.zeros((panel_total, trail_total), jnp.float32),
        columns[:, panel_width:],
        (0, col_index * trail_width),
    )
    gram_sum, cross_sum = reduce_products(gram_part, cross_part)
    panel_factor, coupling, weights = factor_panel(gram_sum, cross_sum, total_rows)
    coupling_own = lax.dynamic_slice_in_dim(coupling, col_index * trail_width, trail_width, 1)
    weights_own = lax.dynamic_slice_in_dim(weights, col_index * trail_width, trail_width, 1)
    weight_high, weight_low = split_weights(weights_own)
    segment = lax.all_gather(panel_own, "col", axis=0, tiled=True)
    trail_residual = (
        trail_own.astype(jnp.float32)
        - contract_cols(weight_high, segment)
        - contract_cols(weight_low, segment)
    )
    cross_factor = coupling_own.T
    return (panel_factor, cross_factor, trail_residual)


def solution(mesh):
    return jax.shard_map(
        per_device,
        mesh=mesh,
        in_specs=(
            P(("row", "col"), None),
            P(None, None, ("row", "col"), None),
            P("col", None),
            P("col", None),
            P(("row", "col"), None),
            P(("row", "col"), None),
            P(("row", "col"), None, None),
        ),
        out_specs=(P(), P("col", None), P("col", "row")),
        check_vma=False,
    )
```

profile of v0, /device:TPU:1, one launch (start us, length us, event | category | flops | bytes accessed | tf_op | source)
XLA Modules:
  0.0 593.3 jit_solution(4389010923176962485)
XLA Ops:
  14.9 55.6 %all-gather.3.cloned.1.call-done = bf16[2560,1024]{1,0:T(8,128)(2,1)} async-done(((bf16[160,1024]{1,0:T(8,128)(2,1)}), bf16[2560,1024]{1,0:T(8,128)(2,1)}) %all-gather.3.cloned.1.call-update) | async-done | bytes 5242896 | tf_op jit(solution)/shard_map/all_gather | solution.py:113
  70.5 5.5 multiply_reduce_fusion.1
  75.9 7.7 %gather_fusion = f32[512,2560]{1,0:T(8,128)} fusion(f32[2560,128]{0,1:T(8,128)} %get-tuple-element.64, s32[1024]{0:T(1024)S(1)} %pad_clamp_fusion.1), kind=kCustom, calls=%fused_computation | custom fusion | bytes 10487808 | tf_op jit(solution)/shard_map/jit(_take)/gather | solution.py:28
  83.6 7.1 %gather.17 = f32[2560,8,16,4]{0,3,2,1:T(4,128)} reshape(f32[2560,512]{0,1:T(8,128)} %bitcast.121) | data formatting | bytes 10485760 | tf_op jit(solution)/shard_map/jit(_take)/gather | solution.py:28
  90.7 4.6 fusion.1
  95.4 12.1 %multiply_reduce_fusion = f32[2560,3,8,16]{0,3,2,1:T(8,128)S(1)} fusion(f32[2560,4,8,16]{0,3,2,1:T(8,128)S(1)} %fusion.1, bf16[3,4,8,16,1024]{4,3,2,1,0:T(8,128)(2,1)S(1)} %bitcast.117, bf16[2560,1024]{1,0:T(8,128)(2,1)} %all-gather.3.cloned.1.call-done), kind=kOutput, calls=%fused_computation.4 | convolution fusion | flops 8059944960 | bytes 17563648 | tf_op jit(solution)/shard_map/dot_general | solution.py:17
  112.8 8.5 %gather.19 = bf16[16,160,8,64]{1,0,3,2:T(8,128)(2,1)} reshape(bf16[2560,8,64]{0,2,1:T(8,128)(2,1)} %bitcast.120) | data formatting | bytes 5242880 | tf_op jit(solution)/shard_map/jit(_take)/gather | solution.py:40
  121.2 3.6 copy_select_fusion.1
  128.9 21.1 %all_to_all.10 = bf16[128,2,1024]{2,1,0:T(2,128)(2,1)S(1)} all-to-all(bf16[128,2,1024]{2,1,0:T(2,128)(2,1)S(1)} %reshape.290), channel_id=1, replica_groups=mesh['row'=8,'col'=16] {'row','col'}, dimensions={0} | all-to-all | bytes 1048576 | tf_op jit(solution)/shard_map/all_to_all | solution.py:124
  152.9 4.3 slice.149
  157.3 4.8 all-to-all-start.1
  162.2 36.1 %all-to-all-done.1 = bf16[128,128,64]{1,2,0:T(8,128)(2,1)S(1)} async-done(((bf16[128,128,64]{1,2,0:T(8,128)(2,1)}), bf16[128,128,64]{1,2,0:T(8,128)(2,1)S(1)}, u32[]{:S(2)}, u32[]{:S(2)}) %all-to-all-start.1) | async-done | bytes 2097184 | tf_op jit(solution)/shard_map/all_to_all | solution.py:131
  199.9 40.1 %all-gather.5.cloned.1.call-done = bf16[512,8192]{1,0:T(8,128)(2,1)} async-done(((bf16[32,8192]{1,0:T(8,128)(2,1)}), bf16[512,8192]{1,0:T(8,128)(2,1)}) %all-gather.5.cloned.1.call-update) | async-done | bytes 8388624 | tf_op jit(solution)/shard_map/all_gather | solution.py:141
  240.1 6.1 %convolution_dynamic-update-slice_fusion.3 = f32[512,512]{0,1:T(8,128)S(1)} fusion(f32[512,512]{0,1:T(8,128)S(1)} %broadcast_in_dim.40, s32[]{:T(128)S(6)} %select_n.80, bf16[512,8192]{1,0:T(8,128)(2,1)} %all-gather.5.cloned.1.call-done, bf16[32,8192]{1,0:T(8,128)(2,1)S(1)} %copy-done.8), kind=kOutput, calls=%fused_computation.54 | convolution fusion | flops 268435456 | bytes 8978436 | tf_op jit(solution)/shard_map/dot_general | solution.py:69
  247.2 2.5 broadcast_in_dim.46
  249.8 3.1 convolution_dynamic-update-slice_fusion
  252.9 3.4 copy.81
  256.2 152.8 %all-reduce.4.cloned.1.call-done = (f32[512,512]{0,1:T(8,128)}, f32[512,2048]{1,0:T(8,128)}) async-done(((f32[512,512]{0,1:T(8,128)}, f32[512,2048]{1,0:T(8,128)}), (f32[512,512]{0,1:T(8,128)}, f32[512,2048]{1,0:T(8,128)})) %all-reduce.4.cloned.1.call-update) | async-done | bytes 5242896 | tf_op jit(solution)/shard_map/psum | solution.py:65
  411.1 11.7 %cholesky.103 = f32[128,128]{1,0:T(8,128)S(1)} custom-call(f32[128,128]{1,0:T(8,128)S(1)} %cholesky.263), custom_call_target="Cholesky" | custom-call | tf_op jit(solution)/shard_map/jit(cholesky)/cholesky | solution.py:47
  423.0 9.8 %custom-call.32 = f32[1,128,128]{1,2,0:T(8,128)S(1)} custom-call(f32[1,128,128]{2,1,0:T(8,128)S(1)} %get-tuple-element.62), custom_call_target="InvertDiagBlocksLowerTriangular" | custom-call | tf_op jit(solution)/shard_map/jit(cholesky)/cholesky | solution.py:47
  433.6 11.7 %cholesky.215 = f32[128,128]{1,0:T(8,128)S(1)} custom-call(f32[128,128]{1,0:T(8,128)S(1)} %cholesky.267), custom_call_target="Cholesky" | custom-call | tf_op jit(solution)/shard_map/jit(cholesky)/cholesky | solution.py:47
  445.6 10.0 %custom-call.33 = f32[1,128,128]{1,2,0:T(8,128)S(1)} custom-call(f32[1,128,128]{2,1,0:T(8,128)S(1)} %get-tuple-element.60), custom_call_target="InvertDiagBlocksLowerTriangular" | custom-call | tf_op jit(solution)/shard_map/jit(cholesky)/cholesky | solution.py:47
  456.5 11.7 %cholesky.236 = f32[128,128]{1,0:T(8,128)S(1)} custom-call(f32[128,128]{1,0:T(8,128)S(1)} %cholesky.272), custom_call_target="Cholesky" | custom-call | tf_op jit(solution)/shard_map/jit(cholesky)/cholesky | solution.py:47
  468.4 9.8 %custom-call.34 = f32[1,128,128]{1,2,0:T(8,128)S(1)} custom-call(f32[1,128,128]{2,1,0:T(8,128)S(1)} %get-tuple-element.58), custom_call_target="InvertDiagBlocksLowerTriangular" | custom-call | tf_op jit(solution)/shard_map/jit(cholesky)/cholesky | solution.py:47
  479.0 11.9 %cholesky.253 = f32[128,128]{1,0:T(8,128)S(1)} custom-call(f32[128,128]{1,0:T(8,128)S(1)} %convolution_subtract_fusion.8), custom_call_target="Cholesky" | custom-call | tf_op jit(solution)/shard_map/jit(cholesky)/cholesky | solution.py:47
  493.7 4.8 broadcast_multiply_fusion
  502.3 11.1 %while.1 = (s32[]{:T(128)}, f32[512,512]{0,1:T(8,128)S(1)}, s32[4,2]{0,1:T(2,128)S(1)}, f32[4,128,128]{2,1,0:T(8,128)}, s32[]{:T(128)}) while((s32[]{:T(128)}, f32[512,512]{0,1:T(8,128)S(1)}, s32[4,2]{0,1:T(2,128)S(1)}, f32[4,128,128]{2,1,0:T(8,128)}, s32[]{:T(128)}) %tuple.40), condition=%wide.while_cond, body=%wide.while_body.sunk | while | flops 2 | bytes 393329 | solution.py:48
  513.5 40.2 %custom-call.35 = f32[4,128,128]{1,2,0:T(8,128)S(1)} custom-call(f32[4,128,128]{2,1,0:T(8,128)} %get-tuple-element.10), custom_call_target="InvertDiagBlocksLowerTriangular" | custom-call | tf_op jit(solution)/shard_map/triangular_solve | solution.py:48
  561.8 3.2 fusion.17
  572.9 2.6 convolution_subtract_fusion.2
  576.5 3.1 fusion.14
  582.7 3.6 convolution_subtract_fusion
  (135 shorter events, 62.8 us)
Async XLA Ops:
  7.2 88.2 %copy-start = (bf16[3,4,128,1024]{3,2,1,0:T(8,128)(2,1)S(1)}, bf16[3,4,128,1024]{3,2,1,0:T(8,128)(2,1)}, u32[]{:S(2)}) copy-start(bf16[3,4,128,1024]{3,2,1,0:T(8,128)(2,1)} %param.8) | copy-start | bytes 9437188
  7.2 63.3 %all-gather.3.cloned.1.call-start = ((), (), s32[]{:S(2)}) async-start(), calls=%async_computation.2 | async-start | bytes 5570560 | tf_op jit(solution)/shard_map/all_gather | solution.py:113
  9.1 230.9 %all-gather.5.cloned.1.call-start = ((), (), s32[]{:S(2)}) async-start(), calls=%async_computation.3 | async-start | bytes 8912896 | tf_op jit(solution)/shard_map/all_gather | solution.py:141
  124.9 2.0 copy-start.5
  157.3 82.8 %copy-start.8 = (bf16[32,8192]{1,0:T(8,128)(2,1)S(1)}, bf16[32,8192]{1,0:T(8,128)(2,1)}, u32[]{:S(2)}) copy-start(bf16[32,8192]{1,0:T(8,128)(2,1)} %reshape.250) | copy-start | bytes 1572868
  157.3 41.0 %all-to-all-start.1 = ((bf16[128,128,64]{1,2,0:T(8,128)(2,1)}), bf16[128,128,64]{1,2,0:T(8,128)(2,1)S(1)}, u32[]{:S(2)}, u32[]{:S(2)}) async-start(bf16[128,128,64]{1,2,0:T(8,128)(2,1)} %bitcast.123), calls=%async_computation.1 | async-start | bytes 4194304 | tf_op jit(solution)/shard_map/all_to_all | solution.py:131
  162.1 246.9 %all-reduce.4.cloned.1.call-start = ((), (), s32[]{:S(2)}) async-start(), calls=%async_computation.4 | async-start | bytes 10485760 | tf_op jit(solution)/shard_map/psum | solution.py:65
  240.1 9.7 %copy-start.2 = (bf16[512,8192]{1,0:T(8,128)(2,1)S(1)}, bf16[512,8192]{1,0:T(8,128)(2,1)}, u32[]{:S(2)}) copy-start(bf16[512,8192]{1,0:T(8,128)(2,1)} %all-gather.5.cloned.1.call-done) | copy-start | bytes 25165828
  246.2 1.0 copy-start.11
  247.2 2.5 copy-start.7
  409.0 1.8 copy-start.10
  513.5 45.9 %copy-start.9 = (f32[512,512]{0,1:T(8,128)}, f32[512,512]{0,1:T(8,128)S(1)}, u32[]{:S(2)}) copy-start(f32[512,512]{0,1:T(8,128)S(1)} %get-tuple-element.126) | copy-start | bytes 3145732
  553.7 5.8 copy-start.4
  561.8 4.3 copy-start.3
  572.9 7.8 %slice-start = ((s8[8388608]{0:T(1024)(128)(4,1)}), s8[4194304]{0:T(1024)(128)(4,1)S(1)}, s32[]{:S(2)}) async-start(s8[8388608]{0:T(1024)(128)(4,1)} %bitcast.118), calls=%async_computation.5 | async-start | bytes 8388608
  576.5 4.2 slice-start.1
  579.6 1.6 copy-start.6
  582.7 3.6 copy-start.1
Sparse Core Ops, SparseCore 0:
  10.8 59.6 all-gather.2
  153.0 86.8 all-gather.4
  253.0 156.0 all-reduce.3
where the time goes:
time: 604 us; the launch traced here: 593 us
  waiting for transfers between devices  285 us (47%)
  other arithmetic  145 us (24%)
  local copies, waits for them, and re-layouts  61.7 us (10%)
  matrix products  58.4 us (10%)
  blocking collectives  21.1 us (3%)
  between operations  17.4 us (3%)
    psum x1, waiting for transfers between devices, reduce_products(): return lax.psum((gram_part, cross_part), ('row', 'col'))  153 us
    another operation x15, other arithmetic, factor_panel(): lower_factor = jnp.linalg.cholesky(gram_matrix)  79.5 us
    all_gather x1, waiting for transfers between devices, per_device(): lax.all_gather(own_envs, 'col', axis=0, tiled=True)  55.6 us
    another operation x3, other arithmetic, factor_panel(): lax.linalg.triangular_solve(lower_factor, cross_sum / total_rows, left_si...  41.4 us
    all_gather x1, waiting for transfers between devices, per_device(): segment = lax.all_gather(panel_own, 'col', axis=0, tiled=True)  40.1 us
    all_to_all x1, waiting for transfers between devices, per_device(): lax.all_to_all(arrange_direct(trail_rows, row_count, col_count), ('row',...  36.1 us
    all_to_all x1, blocking collectives, per_device(): lax.all_to_all(arrange_direct(panel_rows, row_count, col_count), ('row',...  21.1 us
    gather x2, local copies, waits for them, and re-layouts, slot_rows(): jnp.take(correlation, flat_index, axis=1)  14.8 us
  transfers between devices with their start and end apart: 4, of which 4 were waited for; matrix products, arithmetic and copies ran while one was open for 3% of the time, Pallas kernels for 0%

commit v1 on v0

--- a/solution.py
+++ b/solution.py
@@ -4,6 +4,22 @@
 from jax.sharding import PartitionSpec as P
 
 ridge_value = 0.1
+
+
+def collect(x, axis, dim):
+    ways, here, step = (lax.axis_size(axis), lax.axis_index(axis), x.shape[dim])
+    dims = [n * ways if d == dim else n for d, n in enumerate(x.shape)]
+    full = lax.dynamic_update_slice_in_dim(jnp.zeros(dims, x.dtype), x, here * step, axis=dim)
+    going_up = going_down = x
+    for far in range(1, ways // 2 + 1):
+        going_up = lax.ppermute(going_up, axis, [(d, (d + 1) % ways) for d in range(ways)])
+        full = lax.dynamic_update_slice_in_dim(full, going_up, (here - far) % ways * step, axis=dim)
+        if 2 * far < ways:
+            going_down = lax.ppermute(going_down, axis, [(d, (d - 1) % ways) for d in range(ways)])
+            full = lax.dynamic_update_slice_in_dim(
+                full, going_down, (here + far) % ways * step, axis=dim
+            )
+    return full
 
 
 def slot_rows(environments, desc_here, slope_here, count_here, neighbor_here, owner_here):
@@ -138,7 +154,7 @@
     )
     panel_own = restore_direct(received[0], row_count, col_count)
     trail_own = restore_direct(received[1], row_count, col_count)
-    segment = lax.all_gather(panel_own, "col", axis=0, tiled=True)
+    segment = collect(panel_own, "col", 0)
     columns = jnp.concatenate(
         [contract_rows(segment, panel_own), contract_rows(segment, trail_own)], axis=1
     )

time: 604 us -> 658 us (1.089)
  starting transfers between devices: 4.96 us -> 47.3 us
  local copies, waits for them, and re-layouts: 61.7 us -> 87.9 us
  blocking collectives: 21.1 us -> 0 us
    ppermute x0 -> x15, waiting for transfers between devices: none -> 70.7 us  [the longest x8 70.6 us: collect(): lax.ppermute(going_up, axis, [(d, (d + 1) % ways) for d in range(ways)])]
    all_gather x1, waiting for transfers between devices: 40.1 us -> 0.01 us  [per_device(): segment = lax.all_gather(panel_own, 'col', axis=0, tiled=True)]
    all_to_all x1, waiting for transfers between devices: 36.1 us -> 0.01 us  [per_device(): lax.all_to_all(arrange_direct(trail_rows, row_count, col_count), ('row',...]
    ppermute x0 -> x15, starting transfers between devices: none -> 34.6 us  [the longest x7 32.7 us: collect(): lax.ppermute(going_down, axis, [(d, (d - 1) % ways) for d in range(ways)])]
    all_to_all x1 -> x0, blocking collectives: 21.1 us -> none  [per_device(): lax.all_to_all(arrange_direct(panel_rows, row_count, col_count), ('row',...]
    dynamic_update_slice x0 -> x16, local copies, waits for them, and re-layouts: none -> 16.5 us  [the longest x8 8.81 us: collect(): lax.dynamic_update_slice_in_dim(full, going_up, (here - far) % ways * ste...]
    all_to_all x0 -> x1, waiting for transfers between devices: none -> 8.77 us  [per_device(): lax.all_to_all(arrange_direct(panel_rows, row_count, col_count), ('row',...]
    all_to_all x0 -> x1, starting transfers between devices: none -> 7.87 us  [per_device(): lax.all_to_all(arrange_direct(panel_rows, row_count, col_count), ('row',...]
  transfers between devices with their start and end apart: 4 -> 20, of which waited for: 4 -> 11; matrix products, arithmetic and copies ran while one was open for 3% -> 31% of each run, Pallas kernels for 0% -> 0%
where the time goes in v1:
time: 658 us; the launch traced here: 647 us
  waiting for transfers between devices  291 us (44%)
  other arithmetic  142 us (22%)
  local copies, waits for them, and re-layouts  87.9 us (13%)
  matrix products  61.4 us (9%)
  starting transfers between devices  47.3 us (7%)
  between operations  17.7 us (3%)
    psum x1, waiting for transfers between devices, reduce_products(): return lax.psum((gram_part, cross_part), ('row', 'col'))  155 us
    another operation x15, other arithmetic, factor_panel(): lower_factor = jnp.linalg.cholesky(gram_matrix)  79.3 us
    ppermute x8, waiting for transfers between devices, collect(): lax.ppermute(going_up, axis, [(d, (d + 1) % ways) for d in range(ways)])  70.6 us
    all_gather x1, waiting for transfers between devices, per_device(): lax.all_gather(own_envs, 'col', axis=0, tiled=True)  55.7 us
    another operation x3, other arithmetic, factor_panel(): lax.linalg.triangular_solve(lower_factor, cross_sum / total_rows, left_si...  41.4 us
    ppermute x7, starting transfers between devices, collect(): lax.ppermute(going_down, axis, [(d, (d - 1) % ways) for d in range(ways)])  32.7 us
    gather x2, local copies, waits for them, and re-layouts, slot_rows(): jnp.take(correlation, flat_index, axis=1)  14.8 us
  transfers between devices with their start and end apart: 20, of which 11 were waited for; matrix products, arithmetic and copies ran while one was open for 31% of the time, Pallas kernels for 0%

profile of v1, /device:TPU:1, one launch (start us, length us, event | category | flops | bytes accessed | tf_op | source)
XLA Modules:
  0.0 646.9 jit_solution(4234838282801540895)
XLA Ops:
  14.8 55.7 %all-gather.3.cloned.1.call-done = bf16[2560,1024]{1,0:T(8,128)(2,1)} async-done(((bf16[160,1024]{1,0:T(8,128)(2,1)}), bf16[2560,1024]{1,0:T(8,128)(2,1)}) %all-gather.3.cloned.1.call-update) | async-done | bytes 5242896 | tf_op jit(solution)/shard_map/all_gather | solution.py:129
  70.5 5.5 multiply_reduce_fusion.1
  75.9 7.7 %gather_fusion = f32[512,2560]{1,0:T(8,128)} fusion(f32[2560,128]{0,1:T(8,128)} %get-tuple-element.71, s32[1024]{0:T(1024)S(1)} %pad_clamp_fusion.1), kind=kCustom, calls=%fused_computation | custom fusion | bytes 10487808 | tf_op jit(solution)/shard_map/jit(_take)/gather | solution.py:44
  83.6 7.1 %gather.17 = f32[2560,8,16,4]{0,3,2,1:T(4,128)} reshape(f32[2560,512]{0,1:T(8,128)} %bitcast.118) | data formatting | bytes 10485760 | tf_op jit(solution)/shard_map/jit(_take)/gather | solution.py:44
  95.4 12.1 %multiply_reduce_fusion = f32[2560,3,8,16]{0,3,2,1:T(8,128)S(1)} fusion(f32[2560,4,8,16]{0,3,2,1:T(8,128)S(1)} %fusion.1, bf16[3,4,8,16,1024]{4,3,2,1,0:T(8,128)(2,1)S(1)} %bitcast.116, bf16[2560,1024]{1,0:T(8,128)(2,1)} %all-gather.3.cloned.1.call-done), kind=kOutput, calls=%fused_computation.4 | convolution fusion | flops 8059944960 | bytes 17563648 | tf_op jit(solution)/shard_map/dot_general | solution.py:33
  112.8 8.5 %gather.19 = bf16[16,160,8,64]{1,0,3,2:T(8,128)(2,1)} reshape(bf16[2560,8,64]{0,2,1:T(8,128)(2,1)} %bitcast.117) | data formatting | bytes 5242880 | tf_op jit(solution)/shard_map/jit(_take)/gather | solution.py:56
  129.7 7.9 %all-to-all-start = ((bf16[128,2,1024]{2,1,0:T(2,128)(2,1)}), bf16[128,2,1024]{2,1,0:T(2,128)(2,1)S(1)}, u32[]{:S(2)}, u32[]{:S(2)}) async-start(bf16[128,2,1024]{2,1,0:T(2,128)(2,1)} %reshape.290), calls=%async_computation | async-start | bytes 1048576 | tf_op jit(solution)/shard_map/all_to_all | solution.py:140
  142.2 8.8 %all-to-all-done = bf16[128,2,1024]{2,1,0:T(2,128)(2,1)S(1)} async-done(((bf16[128,2,1024]{2,1,0:T(2,128)(2,1)}), bf16[128,2,1024]{2,1,0:T(2,128)(2,1)S(1)}, u32[]{:S(2)}, u32[]{:S(2)}) %all-to-all-start) | async-done | bytes 524320 | tf_op jit(solution)/shard_map/all_to_all | solution.py:140
  173.1 23.2 %collective-permute-done = bf16[32,8192]{1,0:T(8,128)(2,1)S(1)} collective-permute-done((bf16[32,8192]{1,0:T(8,128)(2,1)S(1)}, bf16[32,8192]{1,0:T(8,128)(2,1)S(1)}, u32[]{:S(2)}, u32[]{:S(2)}) %collective-permute-start) | collective-permute-done | bytes 524320 | tf_op jit(solution)/shard_map/ppermute | solution.py:15
  196.3 4.8 collective-permute-start.3
  202.8 9.6 %collective-permute-done.2 = bf16[32,8192]{1,0:T(8,128)(2,1)} collective-permute-done((bf16[32,8192]{1,0:T(8,128)(2,1)S(1)}, bf16[32,8192]{1,0:T(8,128)(2,1)}, u32[]{:S(2)}, u32[]{:S(2)}) %collective-permute-start.2) | collective-permute-done | bytes 524320 | tf_op jit(solution)/shard_map/ppermute | solution.py:15
  212.4 4.8 collective-permute-start.5
  236.5 5.8 collective-permute-done.6
  242.4 4.8 collective-permute-start.9
  248.8 6.8 %collective-permute-done.8 = bf16[32,8192]{1,0:T(8,128)(2,1)S(1)} collective-permute-done((bf16[32,8192]{1,0:T(8,128)(2,1)S(1)}, bf16[32,8192]{1,0:T(8,128)(2,1)S(1)}, u32[]{:S(2)}, u32[]{:S(2)}) %collective-permute-start.8) | collective-permute-done | bytes 524320 | tf_op jit(solution)/shard_map/ppermute | solution.py:15
  255.6 4.8 collective-permute-start.11
  262.1 5.9 collective-permute-done.10
  274.4 4.9 collective-permute-done.12
  280.9 9.8 %collective-permute-done.14 = bf16[32,8192]{1,0:T(8,128)(2,1)S(1)} collective-permute-done((bf16[32,8192]{1,0:T(8,128)(2,1)S(1)}, bf16[32,8192]{1,0:T(8,128)(2,1)S(1)}, u32[]{:S(2)}, u32[]{:S(2)}) %collective-permute-start.14) | collective-permute-done | bytes 524320 | tf_op jit(solution)/shard_map/ppermute | solution.py:15
  291.7 6.0 convolution_dynamic-update-slice_fusion.3
  301.2 6.4 convolution_dynamic-update-slice_fusion
  311.7 154.9 %all-reduce.4.cloned.1.call-done = (f32[512,512]{0,1:T(8,128)}, f32[512,2048]{1,0:T(8,128)}) async-done(((f32[512,512]{0,1:T(8,128)}, f32[512,2048]{1,0:T(8,128)}), (f32[512,512]{0,1:T(8,128)}, f32[512,2048]{1,0:T(8,128)})) %all-reduce.4.cloned.1.call-update) | async-done | bytes 5242896 | tf_op jit(solution)/shard_map/psum | solution.py:81
  468.6 11.7 %cholesky.103 = f32[128,128]{1,0:T(8,128)S(1)} custom-call(f32[128,128]{1,0:T(8,128)S(1)} %cholesky.263), custom_call_target="Cholesky" | custom-call | tf_op jit(solution)/shard_map/jit(cholesky)/cholesky | solution.py:63
  480.5 9.8 %custom-call.32 = f32[1,128,128]{1,2,0:T(8,128)S(1)} custom-call(f32[1,128,128]{2,1,0:T(8,128)S(1)} %get-tuple-element.69), custom_call_target="InvertDiagBlocksLowerTriangular" | custom-call | tf_op jit(solution)/shard_map/jit(cholesky)/cholesky | solution.py:63
  491.1 11.7 %cholesky.215 = f32[128,128]{1,0:T(8,128)S(1)} custom-call(f32[128,128]{1,0:T(8,128)S(1)} %cholesky.267), custom_call_target="Cholesky" | custom-call | tf_op jit(solution)/shard_map/jit(cholesky)/cholesky | solution.py:63
  503.1 10.0 %custom-call.33 = f32[1,128,128]{1,2,0:T(8,128)S(1)} custom-call(f32[1,128,128]{2,1,0:T(8,128)S(1)} %get-tuple-element.67), custom_call_target="InvertDiagBlocksLowerTriangular" | custom-call | tf_op jit(solution)/shard_map/jit(cholesky)/cholesky | solution.py:63
  514.0 11.7 %cholesky.236 = f32[128,128]{1,0:T(8,128)S(1)} custom-call(f32[128,128]{1,0:T(8,128)S(1)} %cholesky.272), custom_call_target="Cholesky" | custom-call | tf_op jit(solution)/shard_map/jit(cholesky)/cholesky | solution.py:63
  525.9 9.8 %custom-call.34 = f32[1,128,128]{1,2,0:T(8,128)S(1)} custom-call(f32[1,128,128]{2,1,0:T(8,128)S(1)} %get-tuple-element.65), custom_call_target="InvertDiagBlocksLowerTriangular" | custom-call | tf_op jit(solution)/shard_map/jit(cholesky)/cholesky | solution.py:63
  536.5 11.9 %cholesky.253 = f32[128,128]{1,0:T(8,128)S(1)} custom-call(f32[128,128]{1,0:T(8,128)S(1)} %convolution_subtract_fusion.8), custom_call_target="Cholesky" | custom-call | tf_op jit(solution)/shard_map/jit(cholesky)/cholesky | solution.py:63
  554.9 11.3 %while.1 = (s32[]{:T(128)}, f32[512,512]{0,1:T(8,128)S(1)}, s32[4,2]{0,1:T(2,128)S(1)}, f32[4,128,128]{2,1,0:T(8,128)}, s32[]{:T(128)}) while((s32[]{:T(128)}, f32[512,512]{0,1:T(8,128)S(1)}, s32[4,2]{0,1:T(2,128)S(1)}, f32[4,128,128]{2,1,0:T(8,128)}, s32[]{:T(128)}) %tuple.42), condition=%wide.while_cond, body=%wide.while_body.sunk | while | flops 2 | bytes 393829 | solution.py:64
  566.3 40.2 %custom-call.35 = f32[4,128,128]{1,2,0:T(8,128)S(1)} custom-call(f32[4,128,128]{2,1,0:T(8,128)} %get-tuple-element.10), custom_call_target="InvertDiagBlocksLowerTriangular" | custom-call | tf_op jit(solution)/shard_map/triangular_solve | solution.py:64
  630.0 5.6 convolution_subtract_fusion.1
  (172 shorter events, 141.4 us)
Async XLA Ops:
  7.2 88.2 %copy-start = (bf16[3,4,128,1024]{3,2,1,0:T(8,128)(2,1)S(1)}, bf16[3,4,128,1024]{3,2,1,0:T(8,128)(2,1)}, u32[]{:S(2)}) copy-start(bf16[3,4,128,1024]{3,2,1,0:T(8,128)(2,1)} %param.8) | copy-start | bytes 9437188
  7.2 63.3 %all-gather.3.cloned.1.call-start = ((), (), s32[]{:S(2)}) async-start(), calls=%async_computation.2 | async-start | bytes 5570560 | tf_op jit(solution)/shard_map/all_gather | solution.py:129
  124.9 2.0 copy-start.3
  129.7 21.3 %all-to-all-start = ((bf16[128,2,1024]{2,1,0:T(2,128)(2,1)}), bf16[128,2,1024]{2,1,0:T(2,128)(2,1)S(1)}, u32[]{:S(2)}, u32[]{:S(2)}) async-start(bf16[128,2,1024]{2,1,0:T(2,128)(2,1)} %reshape.290), calls=%async_computation | async-start | bytes 1048576 | tf_op jit(solution)/shard_map/all_to_all | solution.py:140
  151.0 68.9 %all-to-all-start.1 = ((bf16[128,128,64]{1,2,0:T(8,128)(2,1)}), bf16[128,128,64]{1,2,0:T(8,128)(2,1)S(1)}, u32[]{:S(2)}, u32[]{:S(2)}) async-start(bf16[128,128,64]{1,2,0:T(8,128)(2,1)} %bitcast.29), calls=%async_computation.1 | async-start | bytes 4194304 | tf_op jit(solution)/shard_map/all_to_all | solution.py:147
  155.7 310.9 %all-reduce.4.cloned.1.call-start = ((), (), s32[]{:S(2)}) async-start(), calls=%async_computation.4 | async-start | bytes 10485760 | tf_op jit(solution)/shard_map/psum | solution.py:81
  162.3 129.4 %copy-start.4 = (bf16[32,8192]{1,0:T(8,128)(2,1)}, bf16[32,8192]{1,0:T(8,128)(2,1)S(1)}, u32[]{:S(2)}) copy-start(bf16[32,8192]{1,0:T(8,128)(2,1)S(1)} %reshape.250) | copy-start | bytes 1572868
  162.3 34.0 %collective-permute-start = (bf16[32,8192]{1,0:T(8,128)(2,1)S(1)}, bf16[32,8192]{1,0:T(8,128)(2,1)S(1)}, u32[]{:S(2)}, u32[]{:S(2)}) collective-permute-start(bf16[32,8192]{1,0:T(8,128)(2,1)S(1)} %reshape.250), channel_id=1, source_target_pairs={{0,1},{1,2},{2,3},{3,4},{4,5},{5,6},{6,7},{7,8},{8,9},{9,10},{10,1... | collective-permute-start | bytes 1572872 | tf_op jit(solution)/shard_map/ppermute | solution.py:15
  164.0 32.3 %collective-permute-start.1 = (bf16[32,8192]{1,0:T(8,128)(2,1)S(1)}, bf16[32,8192]{1,0:T(8,128)(2,1)S(1)}, u32[]{:S(2)}, u32[]{:S(2)}) collective-permute-start(bf16[32,8192]{1,0:T(8,128)(2,1)S(1)} %reshape.250), channel_id=1, source_target_pairs={{0,15},{1,0},{2,1},{3,2},{4,3},{5,4},{6,5},{7,6},{8,7},{9,8},{10,9... | collective-permute-start | bytes 1572872 | tf_op jit(solution)/shard_map/ppermute | solution.py:18
  196.3 16.1 %collective-permute-start.2 = (bf16[32,8192]{1,0:T(8,128)(2,1)S(1)}, bf16[32,8192]{1,0:T(8,128)(2,1)}, u32[]{:S(2)}, u32[]{:S(2)}) collective-permute-start(bf16[32,8192]{1,0:T(8,128)(2,1)S(1)} %collective-permute-done), channel_id=1, source_target_pairs={{0,1},{1,2},{2,3},{3,4},{4,5},{5,6},{6,7},{7,8},{8,9},{9,10},{10,1... | collective-permute-start | bytes 1572872 | tf_op jit(solution)/shard_map/ppermute | solution.py:15
  196.3 16.1 %collective-permute-start.3 = (bf16[32,8192]{1,0:T(8,128)(2,1)S(1)}, bf16[32,8192]{1,0:T(8,128)(2,1)S(1)}, u32[]{:S(2)}, u32[]{:S(2)}) collective-permute-start(bf16[32,8192]{1,0:T(8,128)(2,1)S(1)} %collective-permute-done.1), channel_id=1, source_target_pairs={{0,15},{1,0},{2,1},{3,2},{4,3},{5,4},{6,5},{7,6},{8,7},{9,8},{10,9... | collective-permute-start | bytes 1572872 | tf_op jit(solution)/shard_map/ppermute | solution.py:18
  212.4 15.4 %collective-permute-start.4 = (bf16[32,8192]{1,0:T(8,128)(2,1)}, bf16[32,8192]{1,0:T(8,128)(2,1)}, u32[]{:S(2)}, u32[]{:S(2)}) collective-permute-start(bf16[32,8192]{1,0:T(8,128)(2,1)} %collective-permute-done.2), channel_id=1, source_target_pairs={{0,1},{1,2},{2,3},{3,4},{4,5},{5,6},{6,7},{7,8},{8,9},{9,10},{10,1... | collective-permute-start | bytes 1572872 | tf_op jit(solution)/shard_map/ppermute | solution.py:15
  212.4 15.6 %collective-permute-start.5 = (bf16[32,8192]{1,0:T(8,128)(2,1)S(1)}, bf16[32,8192]{1,0:T(8,128)(2,1)}, u32[]{:S(2)}, u32[]{:S(2)}) collective-permute-start(bf16[32,8192]{1,0:T(8,128)(2,1)S(1)} %collective-permute-done.3), channel_id=1, source_target_pairs={{0,15},{1,0},{2,1},{3,2},{4,3},{5,4},{6,5},{7,6},{8,7},{9,8},{10,9... | collective-permute-start | bytes 1572872 | tf_op jit(solution)/shard_map/ppermute | solution.py:18
  219.9 1.3 copy-start.5
  227.8 14.6 %collective-permute-start.6 = (bf16[32,8192]{1,0:T(8,128)(2,1)}, bf16[32,8192]{1,0:T(8,128)(2,1)S(1)}, u32[]{:S(2)}, u32[]{:S(2)}) collective-permute-start(bf16[32,8192]{1,0:T(8,128)(2,1)} %collective-permute-done.4), channel_id=1, source_target_pairs={{0,1},{1,2},{2,3},{3,4},{4,5},{5,6},{6,7},{7,8},{8,9},{9,10},{10,1... | collective-permute-start | bytes 1572872 | tf_op jit(solution)/shard_map/ppermute | solution.py:15
  228.0 14.4 %collective-permute-start.7 = (bf16[32,8192]{1,0:T(8,128)(2,1)}, bf16[32,8192]{1,0:T(8,128)(2,1)S(1)}, u32[]{:S(2)}, u32[]{:S(2)}) collective-permute-start(bf16[32,8192]{1,0:T(8,128)(2,1)} %collective-permute-done.5), channel_id=1, source_target_pairs={{0,15},{1,0},{2,1},{3,2},{4,3},{5,4},{6,5},{7,6},{8,7},{9,8},{10,9... | collective-permute-start | bytes 1572872 | tf_op jit(solution)/shard_map/ppermute | solution.py:18
  242.4 13.2 %collective-permute-start.8 = (bf16[32,8192]{1,0:T(8,128)(2,1)S(1)}, bf16[32,8192]{1,0:T(8,128)(2,1)S(1)}, u32[]{:S(2)}, u32[]{:S(2)}) collective-permute-start(bf16[32,8192]{1,0:T(8,128)(2,1)S(1)} %collective-permute-done.6), channel_id=1, source_target_pairs={{0,1},{1,2},{2,3},{3,4},{4,5},{5,6},{6,7},{7,8},{8,9},{9,10},{10,1... | collective-permute-start | bytes 1572872 | tf_op jit(solution)/shard_map/ppermute | solution.py:15
  242.4 13.2 %collective-permute-start.9 = (bf16[32,8192]{1,0:T(8,128)(2,1)S(1)}, bf16[32,8192]{1,0:T(8,128)(2,1)S(1)}, u32[]{:S(2)}, u32[]{:S(2)}) collective-permute-start(bf16[32,8192]{1,0:T(8,128)(2,1)S(1)} %collective-permute-done.7), channel_id=1, source_target_pairs={{0,15},{1,0},{2,1},{3,2},{4,3},{5,4},{6,5},{7,6},{8,7},{9,8},{10,9... | collective-permute-start | bytes 1572872 | tf_op jit(solution)/shard_map/ppermute | solution.py:18
  255.6 12.3 %collective-permute-start.10 = (bf16[32,8192]{1,0:T(8,128)(2,1)S(1)}, bf16[32,8192]{1,0:T(8,128)(2,1)S(1)}, u32[]{:S(2)}, u32[]{:S(2)}) collective-permute-start(bf16[32,8192]{1,0:T(8,128)(2,1)S(1)} %collective-permute-done.8), channel_id=1, source_target_pairs={{0,1},{1,2},{2,3},{3,4},{4,5},{5,6},{6,7},{7,8},{8,9},{9,10},{10,1... | collective-permute-start | bytes 1572872 | tf_op jit(solution)/shard_map/ppermute | solution.py:15
  255.6 12.3 %collective-permute-start.11 = (bf16[32,8192]{1,0:T(8,128)(2,1)S(1)}, bf16[32,8192]{1,0:T(8,128)(2,1)S(1)}, u32[]{:S(2)}, u32[]{:S(2)}) collective-permute-start(bf16[32,8192]{1,0:T(8,128)(2,1)S(1)} %collective-permute-done.9), channel_id=1, source_target_pairs={{0,15},{1,0},{2,1},{3,2},{4,3},{5,4},{6,5},{7,6},{8,7},{9,8},{10,9... | collective-permute-start | bytes 1572872 | tf_op jit(solution)/shard_map/ppermute | solution.py:18
  267.9 11.4 %collective-permute-start.12 = (bf16[32,8192]{1,0:T(8,128)(2,1)S(1)}, bf16[32,8192]{1,0:T(8,128)(2,1)S(1)}, u32[]{:S(2)}, u32[]{:S(2)}) collective-permute-start(bf16[32,8192]{1,0:T(8,128)(2,1)S(1)} %collective-permute-done.10), channel_id=1, source_target_pairs={{0,1},{1,2},{2,3},{3,4},{4,5},{5,6},{6,7},{7,8},{8,9},{9,10},{10,1... | collective-permute-start | bytes 1572872 | tf_op jit(solution)/shard_map/ppermute | solution.py:15
  267.9 12.2 %collective-permute-start.13 = (bf16[32,8192]{1,0:T(8,128)(2,1)S(1)}, bf16[32,8192]{1,0:T(8,128)(2,1)S(1)}, u32[]{:S(2)}, u32[]{:S(2)}) collective-permute-start(bf16[32,8192]{1,0:T(8,128)(2,1)S(1)} %collective-permute-done.11), channel_id=1, source_target_pairs={{0,15},{1,0},{2,1},{3,2},{4,3},{5,4},{6,5},{7,6},{8,7},{9,8},{10,9... | collective-permute-start | bytes 1572872 | tf_op jit(solution)/shard_map/ppermute | solution.py:18
  279.3 11.4 %collective-permute-start.14 = (bf16[32,8192]{1,0:T(8,128)(2,1)S(1)}, bf16[32,8192]{1,0:T(8,128)(2,1)S(1)}, u32[]{:S(2)}, u32[]{:S(2)}) collective-permute-start(bf16[32,8192]{1,0:T(8,128)(2,1)S(1)} %collective-permute-done.12), channel_id=1, source_target_pairs={{0,1},{1,2},{2,3},{3,4},{4,5},{5,6},{6,7},{7,8},{8,9},{9,10},{10,1... | collective-permute-start | bytes 1572872 | tf_op jit(solution)/shard_map/ppermute | solution.py:15
  297.6 1.0 copy-start.8
  307.6 322.4 %all-gather.5.cloned.1.call-start = ((), (), s32[]{:S(2)}) async-start(), calls=%async_computation.3 | async-start | bytes 8912896 | tf_op jit(solution)/shard_map/all_gather | solution.py:176
  466.6 1.8 copy-start.7
  566.3 48.2 %copy-start.6 = (f32[512,512]{0,1:T(8,128)}, f32[512,512]{0,1:T(8,128)S(1)}, u32[]{:S(2)}) copy-start(f32[512,512]{0,1:T(8,128)S(1)} %get-tuple-element.133) | copy-start | bytes 3145732
  630.0 6.4 copy-start.2
  636.3 3.6 copy-start.1
Sparse Core Ops, SparseCore 0:
  10.8 59.6 all-gather.2
  307.7 158.8 all-reduce.3
  468.7 69.3 all-gather.4
